TPU v7x, 128 devices: a whole 4x4x4 slice. The times are simulated.
128 devices in a mesh: lane: 64 (over z, y, x), ctx: 2 (over core).
Axes of the slice: x: 4, y: 4, z: 4, core: 2. Of those that a mesh axis runs over, the one named last changes fastest.
Arguments:
- view_tokens: bfloat16 [64, 2048, 768], P('lane', 'ctx'), may hold values from -6 to 6
- destinations: int32 [64, 128], P('lane', 'ctx'), may hold values from 0 to 63, as said below
- w_query: bfloat16 [768, 768], replicated, may hold values from -0.21875 to 0.21875
- w_key: bfloat16 [768, 768], replicated, may hold values from -0.21875 to 0.21875
- w_value: bfloat16 [768, 768], replicated, may hold values from -0.21875 to 0.21875
- rate_vector: bfloat16 [768], replicated, may hold values from -0.21875 to 0.21875
- fast_gate: bfloat16 [768, 768], replicated, may hold values from -0.21875 to 0.21875
- fast_up: bfloat16 [768, 768], replicated, may hold values from -0.21875 to 0.21875
- fast_down: bfloat16 [768, 768], replicated, may hold values from -0.21875 to 0.21875
- out_gain: float32 [768], replicated, may hold values from 0.1 to 1.9
Outputs:
- ttt_output: bfloat16 [64, 2048, 768], P('lane', 'ctx')
Inputs may be any that keep to these rules, and one draw needn't show every extreme that they name: `destinations`: for every source device and every segment, the 64 entries name every lane once, except that one lane is named twice and one lane not at all; over all source devices of one segment every lane is named exactly 64 times.
All inputs are finite; a program needn't handle non-finite values.
Results may differ from a plain program's by a relative error of at most 0.012.
Values may be sent and summed in bfloat16 or wider, within the bound.
A program may use at most 128 MiB of HBM per device.

v0:
```python
import functools

import jax
import jax.numpy as jnp
from jax import lax
from jax.experimental import pallas as pl
from jax.experimental.pallas import tpu as pltpu
from jax.sharding import PartitionSpec as P

MESH = pl.DeviceIdType.MESH
LANES = 64
BLK = 16
SIDE = 4
ORDERS = ((2, 1, 0), (0, 2, 1), (1, 0, 2))


def coords_of(lane):
    return (lane // 16, (lane // 4) % 4, lane % 4)


def lane_of(coords):
    return coords[0] * 16 + coords[1] * 4 + coords[2]


def route_kernel(idx_ref, meta_ref, view_ref, buf_ref, all_meta_ref, send, extra, send_sem, recv_sem,
                 ext_send, ext_recv, meta_send, meta_recv, local_sem):
    me = lax.axis_index("lane")
    ctx = lax.axis_index("ctx")
    here = coords_of(me)
    width = view_ref.shape[2]
    part = width // 3

    barrier = pltpu.get_barrier_semaphore()

    def greet(k, carry):
        pl.semaphore_signal(barrier, inc=1, device_id=(lax.rem(me + k, LANES), ctx), device_id_type=MESH)
        return carry

    lax.fori_loop(1, LANES, greet, 0)

    extra[...] = view_ref[idx_ref[LANES]]

    def peer(offset):
        d = coords_of(offset)
        return lane_of([(h + o) % SIDE for h, o in zip(here, d)])

    def pack(k, carry):
        offset = lax.rem(k * 21, LANES)
        send[offset] = view_ref[idx_ref[peer(offset)]]
        return carry

    lax.fori_loop(0, LANES, pack, 0)
    pl.semaphore_wait(barrier, LANES - 1)

    own_extra = pltpu.make_async_copy(extra, buf_ref.at[1, here[0], here[1], here[2]], local_sem.at[0])
    own_prim = pltpu.make_async_copy(send.at[0], buf_ref.at[0, 0, 0, 0], local_sem.at[1])
    own_meta = pltpu.make_async_copy(meta_ref, all_meta_ref.at[here[0], here[1], here[2]], local_sem.at[2])
    own_extra.start()
    own_prim.start()
    own_meta.start()

    def held(p, stage, coords):
        done = ORDERS[p][:stage]
        spot = [pl.ds(0, SIDE) if a in done else coords[a] for a in range(3)]
        return spot

    def ext_copy(p, stage, delta, back):
        axis = ORDERS[p][stage]
        coords = list(here)
        if back:
            coords[axis] = (here[axis] - delta) % SIDE
        z, y, x = held(p, stage, coords)
        slab = buf_ref.at[1, z, y, x, :, pl.ds(p * part, part)]
        source = extra.at[:, pl.ds(p * part, part)] if stage == 0 else slab
        if back:
            source = slab
        to = list(here)
        to[axis] = (here[axis] + delta) % SIDE
        return pltpu.make_async_remote_copy(
            src_ref=source, dst_ref=slab,
            send_sem=ext_send.at[p, stage, delta - 1], recv_sem=ext_recv.at[p, stage, delta - 1],
            device_id=(lane_of(to), ctx), device_id_type=MESH)

    def meta_copy(stage, delta, back):
        axis = ORDERS[0][stage]
        coords = list(here)
        if back:
            coords[axis] = (here[axis] - delta) % SIDE
        z, y, x = held(0, stage, coords)
        slab = all_meta_ref.at[z, y, x]
        to = list(here)
        to[axis] = (here[axis] + delta) % SIDE
        source = meta_ref if stage == 0 and not back else slab
        return pltpu.make_async_remote_copy(
            src_ref=source, dst_ref=slab,
            send_sem=meta_send.at[stage, delta - 1], recv_sem=meta_recv.at[stage, delta - 1],
            device_id=(lane_of(to), ctx), device_id_type=MESH)

    def start_stage(stage):
        for delta in (1, 3, 2):
            meta_copy(stage, delta, False).start()
            for p in range(3):
                ext_copy(p, stage, delta, False).start()

    def end_stage(stage):
        for delta in (1, 3, 2):
            meta_copy(stage, delta, True).wait_recv()
            for p in range(3):
                ext_copy(p, stage, delta, True).wait_recv()

    def post(k, carry):
        offset = lax.rem(k * 21, LANES)
        d = coords_of(offset)
        pltpu.make_async_remote_copy(
            src_ref=send.at[offset], dst_ref=buf_ref.at[0, d[0], d[1], d[2]],
            send_sem=send_sem, recv_sem=recv_sem,
            device_id=(peer(offset), ctx), device_id_type=MESH).start()
        return carry

    start_stage(0)
    lax.fori_loop(1, 22, post, 0)
    own_extra.wait()
    own_meta.wait()
    end_stage(0)
    start_stage(1)
    lax.fori_loop(22, 43, post, 0)
    end_stage(1)
    start_stage(2)
    lax.fori_loop(43, LANES, post, 0)
    end_stage(2)
    own_prim.wait()
    for stage in range(3):
        for delta in (1, 3, 2):
            meta_copy(stage, delta, False).wait_send()
            for p in range(3):
                ext_copy(p, stage, delta, False).wait_send()


    first = pltpu.make_async_remote_copy(
        src_ref=send.at[pl.ds(1, LANES - 1)], dst_ref=send.at[pl.ds(1, LANES - 1)],
        send_sem=send_sem, recv_sem=recv_sem,
        device_id=(peer(1), ctx), device_id_type=MESH)
    first.wait_send()
    first.wait_recv()


def route(idx, meta, blocks):
    width = blocks.shape[2]
    return pl.pallas_call(
        route_kernel,
        out_shape=(
            jax.ShapeDtypeStruct((2, SIDE, SIDE, SIDE, BLK, width), jnp.bfloat16),
            jax.ShapeDtypeStruct((SIDE, SIDE, SIDE, 1, 128), jnp.int32),
        ),
        in_specs=[
            pl.BlockSpec(memory_space=pltpu.SMEM),
            pl.BlockSpec(memory_space=pltpu.VMEM),
            pl.BlockSpec(memory_space=pltpu.VMEM),
        ],
        out_specs=(pl.BlockSpec(memory_space=pl.ANY), pl.BlockSpec(memory_space=pl.ANY)),
        scratch_shapes=[
            pltpu.VMEM((LANES, BLK, width), jnp.bfloat16),
            pltpu.VMEM((BLK, width), jnp.bfloat16),
            pltpu.SemaphoreType.DMA,
            pltpu.SemaphoreType.DMA,
            pltpu.SemaphoreType.DMA((3, 3, 3)),
            pltpu.SemaphoreType.DMA((3, 3, 3)),
            pltpu.SemaphoreType.DMA((3, 3)),
            pltpu.SemaphoreType.DMA((3, 3)),
            pltpu.SemaphoreType.DMA((3,)),
        ],
        compiler_params=pltpu.CompilerParams(
            collective_id=0, has_side_effects=True, vmem_limit_bytes=16 << 20
        ),
        name="route",
    )(idx, meta, blocks)


def project_kernel(meta_ref, buf_ref, wq_ref, wk_ref, wv_ref, rate_ref, q_ref, k_ref, v_ref, tokens, table, sems):
    me = lax.axis_index("lane")
    here = coords_of(me)

    def place(s, p):
        c = coords_of(s)
        slot = lane_of([(h - o) % SIDE for h, o in zip(here, c)])
        table[p] = slot
        p = p + (meta_ref[s, 1] != me).astype(jnp.int32)
        table[p] = s + LANES
        return p + (meta_ref[s, 0] == me).astype(jnp.int32)

    lax.fori_loop(0, LANES, place, jnp.int32(0))
    chunk_blocks = 16
    chunks = LANES // chunk_blocks

    def fetch(r, carry):
        pltpu.make_async_copy(buf_ref.at[table[r]], tokens.at[r], sems.at[r // chunk_blocks]).start()
        return carry

    lax.fori_loop(0, LANES, fetch, 0)

    def project(c, carry):
        span = pl.ds(c * chunk_blocks, chunk_blocks)
        pltpu.make_async_copy(buf_ref.at[span], tokens.at[span], sems.at[c]).wait()
        x = tokens[span].reshape(chunk_blocks * BLK, tokens.shape[2])
        rows = pl.ds(c * chunk_blocks * BLK, chunk_blocks * BLK)
        q = jnp.dot(x, wq_ref[...], preferred_element_type=jnp.float32)
        q_ref[rows, :] = (q * row_scale(q)).astype(jnp.bfloat16)
        k = jnp.dot(x, wk_ref[...], preferred_element_type=jnp.float32)
        k_ref[rows, :] = (k * row_scale(k)).astype(jnp.bfloat16)
        rate = jnp.dot(x, rate_ref[...], preferred_element_type=jnp.float32)
        rate = jnp.maximum(rate, 0.0) + jnp.log1p(jnp.exp(-jnp.abs(rate)))
        v = jnp.dot(x, wv_ref[...], preferred_element_type=jnp.float32)
        v_ref[rows, :] = (rate[:, :1] * v).astype(jnp.bfloat16)
        return carry

    lax.fori_loop(0, chunks, project, 0)


def row_scale(values):
    return lax.rsqrt(jnp.mean(values * values, axis=-1, keepdims=True) + 1e-06)


def project(meta, buf, w_query, w_key, w_value, rate):
    width = buf.shape[2]
    rows = LANES * BLK
    made = jax.ShapeDtypeStruct((rows, width), jnp.bfloat16)
    vmem = pl.BlockSpec(memory_space=pltpu.VMEM)
    return pl.pallas_call(
        project_kernel,
        out_shape=(made, made, made),
        in_specs=[pl.BlockSpec(memory_space=pltpu.SMEM), pl.BlockSpec(memory_space=pl.ANY), vmem, vmem, vmem, vmem],
        out_specs=(vmem, vmem, vmem),
        scratch_shapes=[
            pltpu.VMEM((LANES, BLK, width), jnp.bfloat16),
            pltpu.SMEM((LANES + 8,), jnp.int32),
            pltpu.SemaphoreType.DMA((4,)),
        ],
        compiler_params=pltpu.CompilerParams(vmem_limit_bytes=40 << 20),
        name="project",
    )(meta, buf, w_query, w_key, w_value, rate)


def dot_f32(left_side, right_side):
    return jnp.dot(left_side, right_side, preferred_element_type=jnp.float32)


def contract_rows(left_side, right_side):
    return lax.dot_general(
        left_side, right_side, (((0,), (0,)), ((), ())), preferred_element_type=jnp.float32
    )


def fast_update(gate_w, up_w, down_w, keys_bf, scaled_values):
    gate_pre = dot_f32(keys_bf, gate_w)
    up_pre = dot_f32(keys_bf, up_w)
    gate_sig = jax.nn.sigmoid(gate_pre)
    hidden = (gate_pre * gate_sig * up_pre).astype(jnp.bfloat16)
    back = lax.dot_general(
        scaled_values, down_w, (((1,), (1,)), ((), ())), preferred_element_type=jnp.float32
    )
    gate_term = (back * up_pre * gate_sig * (1.0 + gate_pre * (1.0 - gate_sig))).astype(
        jnp.bfloat16
    )
    up_term = (back * gate_pre * gate_sig).astype(jnp.bfloat16)
    gradients = (
        contract_rows(keys_bf, gate_term),
        contract_rows(keys_bf, up_term),
        contract_rows(hidden, scaled_values),
    )
    step_size = 0.5 * gate_w.shape[0] ** (-0.5)
    renewed = []
    for previous, gradient in zip((gate_w, up_w, down_w), gradients):
        renewed.append(
            (previous.astype(jnp.float32) + step_size * gradient * row_scale(gradient)).astype(
                jnp.bfloat16
            )
        )
    return tuple(renewed)


def apply_queries(gate_w, up_w, down_w, queries_bf, out_gain):
    q_gate = dot_f32(queries_bf, gate_w)
    q_up = dot_f32(queries_bf, up_w)
    q_hidden = (jax.nn.silu(q_gate) * q_up).astype(jnp.bfloat16)
    output_pre = dot_f32(q_hidden, down_w)
    return (output_pre * row_scale(output_pre) * out_gain).astype(jnp.bfloat16)


def body(
    view_tokens,
    destinations,
    w_query,
    w_key,
    w_value,
    rate_vector,
    fast_gate,
    fast_up,
    fast_down,
    out_gain,
):
    position = lax.axis_index("ctx")
    width = view_tokens.shape[2]
    blocks = view_tokens[0].reshape(LANES, BLK, width)
    lane_ids = jnp.arange(LANES, dtype=jnp.int32)
    named = destinations[0][:, None] == lane_ids[None, :]
    first = jnp.min(jnp.where(named, lane_ids[:, None], LANES), axis=0)
    last = jnp.max(jnp.where(named, lane_ids[:, None], -1), axis=0)
    twice = last > first
    extra = jnp.max(jnp.where(twice, last, -1))
    doubled = jnp.max(jnp.where(twice, lane_ids, -1))
    missed = jnp.max(jnp.where(first == LANES, lane_ids, -1))
    columns = jnp.arange(128, dtype=jnp.int32)
    idx = jnp.where(columns < LANES, jnp.pad(jnp.minimum(first, LANES - 1), (0, 64)), extra)
    meta = jnp.where(columns == 0, doubled, missed)[None, :]
    buf, all_meta = route(idx, meta, blocks)
    rate = jnp.broadcast_to(rate_vector[:, None], (width, 128))
    queries, keys, values = project(
        all_meta.reshape(LANES, 128), buf.reshape(2 * LANES, BLK, width), w_query, w_key, w_value, rate
    )
    initial = (fast_gate, fast_up, fast_down)
    updated = fast_update(*initial, keys, values)
    arrived = [lax.ppermute(w, "ctx", [(0, 1)]) for w in updated]
    weights = [jnp.where(position == 0, a, b) for a, b in zip(initial, arrived)]
    weights = fast_update(*weights, keys, values)
    return apply_queries(*weights, queries, out_gain)[None]


def solution(mesh):
    placed = (P("lane", "ctx", None), P("lane", "ctx"), P(), P(), P(), P(), P(), P(), P(), P())
    return jax.shard_map(
        body, mesh=mesh, in_specs=placed, out_specs=P("lane", "ctx", None), check_vma=False
    )
```

profile of v0, /device:TPU:1, one launch (start us, length us, event | category | flops | bytes accessed | tf_op | source)
XLA Modules:
  0.0 125.6 jit_solution(10373658702061667266)
XLA Ops:
  0.9 2.4 %copy.23 = bf16[768,768]{0,1:T(8,128)(2,1)} copy(bf16[768,768]{1,0:T(8,128)(2,1)} %param.17) | data formatting | bytes 2359296 | tf_op args[7]
  5.9 43.9 %route.1 = (bf16[2,4,4,4,16,768]{5,4,3,2,1,0:T(8,128)(2,1)S(1)}, s32[4,4,4,1,128]{4,3,2,1,0:T(1,128)S(1)}) custom-call(s32[128]{0:T(128)S(1)} %compare_select_fusion.2.idx_ref, s32[1,128]{1,0:T(1,128)S(1)} %compare_select_fusion.1.meta_ref, bf16[64,16,768]{2,1,0:T(8,128)(2,1)S(1)} %bitcast.24), custom_call_target="tpu_custom_call" | custom-call | tf_op jit(solution)/shard_map/route/pallas_call | solution.py:149
  51.2 10.4 %project.1 = (bf16[1024,768]{1,0:T(8,128)(2,1)S(1)}, bf16[1024,768]{1,0:T(8,128)(2,1)S(1)}, bf16[1024,768]{1,0:T(8,128)(2,1)S(1)}) custom-call(s32[64,128]{1,0:T(8,128)S(1)} %bitcast.25, bf16[128,16,768]{2,1,0:T(8,128)(2,1)S(1)} %bitcast.23, bf16[768,768]{1,0:T(8,128)(2,1)S(1)} %copy-done.1, bf16[768,768]{1,0:T(8,128)(2,1)S(1)} %copy-done.2, ...), custom_call_target="tpu_custom_call" | custom-call | tf_op jit(solution)/shard_map/project/pallas_call | solution.py:228
  63.8 1.4 %fusion.26 = f32[1024,768]{1,0:T(8,128)S(1)} fusion(bf16[1024,768]{1,0:T(8,128)(2,1)S(1)} %get-tuple-element.14, bf16[768,768]{1,0:T(8,128)(2,1)S(1)} %copy-done.15), kind=kOutput, calls=%fused_computation.67 | convolution fusion | flops 1207959552 | bytes 5898240 | tf_op jit(solution)/shard_map/dot_general | solution.py:258
  65.3 1.9 %multiply_reduce_fusion.4 = (f32[768]{0:T(1024)S(1)}, f32[768,768]{0,1:T(8,128)S(1)}) fusion(bf16[1024,768]{1,0:T(8,128)(2,1)S(1)} %get-tuple-element.13, f32[1024,768]{1,0:T(8,128)S(1)} %fusion.26, f32[1024,768]{1,0:T(8,128)S(1)} %fusion.28), kind=kOutput, calls=%fused_computation.18 | convolution fusion | flops 1213857024 | bytes 10226688 | tf_op jit(solution)/shard_map/dot_general | solution.py:248
  67.4 1.4 %add_convert_fusion.3 = bf16[768,768]{0,1:T(8,128)(2,1)} fusion(f32[768,768]{0,1:T(8,128)S(1)} %get-tuple-element.26, bf16[768,768]{0,1:T(8,128)(2,1)S(1)} %copy-done.11, f32[768]{0:T(1024)S(1)} %rsqrt_multiply_fusion.3), kind=kLoop, calls=%fused_computation.17 | loop fusion | flops 2359296 | bytes 4721664 | tf_op jit(solution)/shard_map/convert_element_type | solution.py:274
  68.8 1.4 %collective-permute-start.2 = (bf16[768,768]{0,1:T(8,128)(2,1)}, bf16[768,768]{0,1:T(8,128)(2,1)}, u32[]{:S(2)}, u32[]{:S(2)}) collective-permute-start(bf16[768,768]{0,1:T(8,128)(2,1)} %add_convert_fusion.3), channel_id=1, source_target_pairs={{0,1},{2,3},{4,5},{6,7},{8,9},{10,11},{12,13},{14,15},{16,17},{18,... | collective-permute-start | bytes 3538952 | tf_op jit(solution)/shard_map/ppermute | solution.py:322
  70.3 2.4 %copy.19 = bf16[768,768]{0,1:T(8,128)(2,1)} copy(bf16[768,768]{1,0:T(8,128)(2,1)} %param.16) | data formatting | bytes 2359296 | tf_op args[6]
  72.7 2.8 %fusion.27 = f32[1024,768]{1,0:T(8,128)S(1)} fusion(bf16[1024,768]{1,0:T(8,128)(2,1)S(1)} %copy-done.5, bf16[768,768]{1,0:T(8,128)(2,1)} %param.17), kind=kOutput, calls=%fused_computation.68 | convolution fusion | flops 1207959552 | bytes 5898240 | tf_op jit(solution)/shard_map/dot_general | solution.py:244
  75.9 2.2 %multiply_reduce_fusion.6 = (f32[768]{0:T(1024)S(1)}, f32[768,768]{0,1:T(8,128)S(1)}) fusion(bf16[1024,768]{1,0:T(8,128)(2,1)S(1)} %copy-done.5, f32[1024,768]{1,0:T(8,128)S(1)} %copy-done.19, f32[1024,768]{1,0:T(8,128)S(1)} %copy-done.21, f32[1024,768]{1,0:T(8,128)S(1)} %fusion.27), kind=kOutput, calls=%fused_computation.22 | convolution fusion | flops 1217002752 | bytes 13372416 | tf_op jit(solution)/shard_map/dot_general | solution.py:248
  80.7 3.2 %multiply_reduce_fusion.5 = (f32[768]{0:T(1024)S(1)}, f32[768,768]{0,1:T(8,128)}) fusion(bf16[1024,768]{1,0:T(8,128)(2,1)S(1)} %copy-done.7, f32[1024,768]{1,0:T(8,128)S(1)} %fusion.27, f32[1024,768]{1,0:T(8,128)S(1)} %copy-done.19), kind=kOutput, calls=%fused_computation.20 | convolution fusion | flops 1213857024 | bytes 10226688 | tf_op jit(solution)/shard_map/dot_general | solution.py:248
  83.9 2.4 %copy.21 = bf16[768,768]{0,1:T(8,128)(2,1)} copy(bf16[768,768]{1,0:T(8,128)(2,1)} %param.18) | data formatting | bytes 2359296 | tf_op args[8]
  86.3 3.3 %add_convert_fusion.4 = bf16[768,768]{0,1:T(8,128)(2,1)} fusion(f32[768,768]{0,1:T(8,128)} %get-tuple-element.24, bf16[768,768]{0,1:T(8,128)(2,1)} %copy.21, f32[768]{0:T(1024)S(1)} %rsqrt_multiply_fusion.4), kind=kLoop, calls=%fused_computation.19 | loop fusion | flops 2359296 | bytes 4721664 | tf_op jit(solution)/shard_map/convert_element_type | solution.py:274
  89.5 1.5 %collective-permute-start.1 = (bf16[768,768]{0,1:T(8,128)(2,1)}, bf16[768,768]{0,1:T(8,128)(2,1)}, u32[]{:S(2)}, u32[]{:S(2)}) collective-permute-start(bf16[768,768]{0,1:T(8,128)(2,1)} %add_convert_fusion.4), channel_id=1, source_target_pairs={{0,1},{2,3},{4,5},{6,7},{8,9},{10,11},{12,13},{14,15},{16,17},{18,... | collective-permute-start | bytes 3538952 | tf_op jit(solution)/shard_map/ppermute | solution.py:322
  91.0 2.8 %fusion.15 = f32[1024,768]{1,0:T(8,128)S(1)} fusion(bf16[1024,768]{1,0:T(8,128)(2,1)S(1)} %copy-done.5, bf16[768,768]{0,1:T(8,128)(2,1)} %copy.23, bf16[768,768]{0,1:T(8,128)(2,1)} %collective-permute-done.2, pred[]{:T(512)S(6)} %eq.47), kind=kOutput, calls=%fused_computation.40 | convolution fusion | flops 1208549376 | bytes 7077889 | tf_op jit(solution)/shard_map/dot_general | solution.py:244
  93.9 2.8 %fusion.13 = f32[1024,768]{1,0:T(8,128)S(1)} fusion(bf16[1024,768]{1,0:T(8,128)(2,1)S(1)} %copy-done.5, bf16[768,768]{0,1:T(8,128)(2,1)S(1)} %copy-done.10, bf16[768,768]{0,1:T(8,128)(2,1)} %collective-permute-done, pred[]{:T(512)S(6)} %eq.47), kind=kOutput, calls=%fused_computation.38 | convolution fusion | flops 1208549376 | bytes 7077889 | tf_op jit(solution)/shard_map/dot_general | solution.py:244
  96.7 3.2 %multiply_reduce_fusion.1 = (f32[768]{0:T(1024)S(1)}, f32[768,768]{0,1:T(8,128)}) fusion(bf16[1024,768]{1,0:T(8,128)(2,1)S(1)} %copy-done.8, f32[1024,768]{1,0:T(8,128)S(1)} %fusion.15, f32[1024,768]{1,0:T(8,128)S(1)} %fusion.13), kind=kOutput, calls=%fused_computation.12 | convolution fusion | flops 1213857024 | bytes 10226688 | tf_op jit(solution)/shard_map/dot_general | solution.py:248
  99.9 2.7 %fusion.14 = f32[1024,768]{1,0:T(8,128)S(1)} fusion(bf16[1024,768]{1,0:T(8,128)(2,1)S(1)} %copy-done.8, bf16[768,768]{0,1:T(8,128)(2,1)S(1)} %copy-done.13, bf16[768,768]{0,1:T(8,128)(2,1)} %collective-permute-done.1, pred[]{:T(512)S(6)} %eq.47), kind=kOutput, calls=%fused_computation.39 | convolution fusion | flops 1208549376 | bytes 7077889 | tf_op jit(solution)/shard_map/dot_general | solution.py:258
  102.6 2.2 %multiply_reduce_fusion.3 = (f32[768]{0:T(1024)S(1)}, f32[768,768]{0,1:T(8,128)S(1)}) fusion(bf16[1024,768]{1,0:T(8,128)(2,1)S(1)} %copy-done.5, f32[1024,768]{1,0:T(8,128)S(1)} %fusion.13, f32[1024,768]{1,0:T(8,128)S(1)} %fusion.14, f32[1024,768]{1,0:T(8,128)S(1)} %fusion.15), kind=kOutput, calls=%fused_computation.16 | convolution fusion | flops 1217002752 | bytes 13372416 | tf_op jit(solution)/shard_map/dot_general | solution.py:248
  104.9 3.3 %multiply_reduce_fusion.2 = (f32[768]{0:T(1024)S(1)}, f32[768,768]{0,1:T(8,128)}) fusion(bf16[1024,768]{1,0:T(8,128)(2,1)S(1)} %copy-done.5, f32[1024,768]{1,0:T(8,128)S(1)} %fusion.14, f32[1024,768]{1,0:T(8,128)S(1)} %fusion.13), kind=kOutput, calls=%fused_computation.14 | convolution fusion | flops 1213857024 | bytes 10226688 | tf_op jit(solution)/shard_map/dot_general | solution.py:248
  108.3 4.5 %fusion.8 = f32[1024,768]{1,0:T(8,128)} fusion(bf16[1024,768]{1,0:T(8,128)(2,1)S(1)} %get-tuple-element.12, f32[768,768]{0,1:T(8,128)S(1)} %get-tuple-element.28, f32[768]{0:T(1024)S(1)} %rsqrt_multiply_fusion.2, bf16[768,768]{0,1:T(8,128)(2,1)S(1)} %copy-done.10, bf16[768,768]{0,1:T(8,128)(2,1)} %collective-permute-done, pred[]{:T(512)S(6)} %eq.47), kind=kOutput, calls=%fused_computation.31 | convolution fusion | flops 1210908672 | bytes 9440257 | tf_op jit(solution)/shard_map/dot_general | solution.py:244
  112.8 9.0 %multiply_reduce_fusion = (f32[1024]{0:T(1024)S(1)}, f32[1024,768]{0,1:T(8,128)}) fusion(f32[768,768]{0,1:T(8,128)} %get-tuple-element.30, f32[768]{0:T(1024)S(1)} %rsqrt_multiply_fusion, bf16[768,768]{0,1:T(8,128)(2,1)} %copy.21, bf16[768,768]{0,1:T(8,128)(2,1)} %collective-permute-done.1, pred[]{:T(512)S(6)} %eq.47, f32[1024,768]{1,0:T(8,128)} %fusion.8, ...), kind=kOutput, calls=%fused_computation.1 | convolution fusion | flops 2428107776 | bytes 17311744 | tf_op jit(solution)/shard_map/dot_general | solution.py:244
  121.8 2.2 %fusion = bf16[1,1024,768]{1,2,0:T(8,128)(2,1)S(1)} fusion(f32[1024,768]{0,1:T(8,128)} %get-tuple-element.34, f32[768]{0:T(1024)S(1)} %copy-done.16, f32[1024]{0:T(1024)S(1)} %add_rsqrt_fusion), kind=kLoop, calls=%fused_computation.23 | loop fusion | flops 2359296 | bytes 4725760 | tf_op jit(solution)/shard_map/broadcast_in_dim | solution.py:325
  124.0 1.6 %copy.24 = bf16[1,1024,768]{2,1,0:T(8,128)(2,1)} copy(bf16[1,1024,768]{1,2,0:T(8,128)(2,1)S(1)} %fusion) | data formatting | bytes 3145728 | tf_op jit(solution)/shard_map/broadcast_in_dim | solution.py:325
  (62 shorter events, 10.3 us)
Async XLA Ops:
  0.0 5.9 %copy-start = (bf16[1,1024,768]{2,1,0:T(8,128)(2,1)S(1)}, bf16[1,1024,768]{2,1,0:T(8,128)(2,1)}, u32[]{:S(2)}) copy-start(bf16[1,1024,768]{2,1,0:T(8,128)(2,1)} %param.10) | copy-start | bytes 4718596
  0.0 49.9 %copy-start.1 = (bf16[768,768]{1,0:T(8,128)(2,1)S(1)}, bf16[768,768]{1,0:T(8,128)(2,1)}, u32[]{:S(2)}) copy-start(bf16[768,768]{1,0:T(8,128)(2,1)} %wq_ref.1) | copy-start | bytes 3538948
  0.0 49.7 %copy-start.17 = (bf16[768]{0:T(1024)(128)(2,1)S(1)}, bf16[768]{0:T(1024)(128)(2,1)}, u32[]{:S(2)}) copy-start(bf16[768]{0:T(1024)(128)(2,1)} %param.15) | copy-start | bytes 4612
  3.3 46.6 %copy-start.2 = (bf16[768,768]{1,0:T(8,128)(2,1)S(1)}, bf16[768,768]{1,0:T(8,128)(2,1)}, u32[]{:S(2)}) copy-start(bf16[768,768]{1,0:T(8,128)(2,1)} %wk_ref.1) | copy-start | bytes 3538948
  51.2 10.4 %copy-start.14 = (bf16[768,768]{1,0:T(8,128)(2,1)S(1)}, bf16[768,768]{1,0:T(8,128)(2,1)}, u32[]{:S(2)}) copy-start(bf16[768,768]{1,0:T(8,128)(2,1)} %param.16) | copy-start | bytes 3538948
  61.6 1.5 %copy-start.6 = (bf16[1024,768]{1,0:T(8,128)(2,1)}, bf16[1024,768]{1,0:T(8,128)(2,1)S(1)}, u32[]{:S(2)}) copy-start(bf16[1024,768]{1,0:T(8,128)(2,1)S(1)} %get-tuple-element.14) | copy-start | bytes 4718596
  61.6 3.6 %copy-start.4 = (bf16[1024,768]{1,0:T(8,128)(2,1)}, bf16[1024,768]{1,0:T(8,128)(2,1)S(1)}, u32[]{:S(2)}) copy-start(bf16[1024,768]{1,0:T(8,128)(2,1)S(1)} %get-tuple-element.13) | copy-start | bytes 4718596
  61.7 2.2 %copy-start.15 = (bf16[768,768]{1,0:T(8,128)(2,1)S(1)}, bf16[768,768]{1,0:T(8,128)(2,1)}, u32[]{:S(2)}) copy-start(bf16[768,768]{1,0:T(8,128)(2,1)} %param.18) | copy-start | bytes 3538948
  63.1 2.2 %copy-start.18 = (f32[1024,768]{1,0:T(8,128)}, f32[1024,768]{1,0:T(8,128)S(1)}, u32[]{:S(2)}) copy-start(f32[1024,768]{1,0:T(8,128)S(1)} %fusion.28) | copy-start | bytes 9437188
  65.3 1.9 %copy-start.20 = (f32[1024,768]{1,0:T(8,128)}, f32[1024,768]{1,0:T(8,128)S(1)}, u32[]{:S(2)}) copy-start(f32[1024,768]{1,0:T(8,128)S(1)} %fusion.26) | copy-start | bytes 9437188
  65.3 2.1 %copy-start.11 = (bf16[768,768]{0,1:T(8,128)(2,1)S(1)}, bf16[768,768]{0,1:T(8,128)(2,1)}, u32[]{:S(2)}) copy-start(bf16[768,768]{0,1:T(8,128)(2,1)} %copy.23) | copy-start | bytes 3538948
  68.8 3.8 %copy-start.5 = (bf16[1024,768]{1,0:T(8,128)(2,1)S(1)}, bf16[1024,768]{1,0:T(8,128)(2,1)}, u32[]{:S(2)}) copy-start(bf16[1024,768]{1,0:T(8,128)(2,1)} %copy-done.4) | copy-start | bytes 4718596
  68.8 22.2 %collective-permute-start.2 = (bf16[768,768]{0,1:T(8,128)(2,1)}, bf16[768,768]{0,1:T(8,128)(2,1)}, u32[]{:S(2)}, u32[]{:S(2)}) collective-permute-start(bf16[768,768]{0,1:T(8,128)(2,1)} %add_convert_fusion.3), channel_id=1, source_target_pairs={{0,1},{2,3},{4,5},{6,7},{8,9},{10,11},{12,13},{14,15},{16,17},{18,... | collective-permute-start | bytes 3538952 | tf_op jit(solution)/shard_map/ppermute | solution.py:322
  72.7 2.8 %copy-start.19 = (f32[1024,768]{1,0:T(8,128)S(1)}, f32[1024,768]{1,0:T(8,128)}, u32[]{:S(2)}) copy-start(f32[1024,768]{1,0:T(8,128)} %copy-done.18) | copy-start | bytes 9437188
  72.7 3.2 %copy-start.21 = (f32[1024,768]{1,0:T(8,128)S(1)}, f32[1024,768]{1,0:T(8,128)}, u32[]{:S(2)}) copy-start(f32[1024,768]{1,0:T(8,128)} %copy-done.20) | copy-start | bytes 9437188
  75.9 2.2 %copy-start.9 = (bf16[768,768]{0,1:T(8,128)(2,1)S(1)}, bf16[768,768]{0,1:T(8,128)(2,1)}, u32[]{:S(2)}) copy-start(bf16[768,768]{0,1:T(8,128)(2,1)} %copy.19) | copy-start | bytes 3538948
  78.1 2.6 %copy-start.7 = (bf16[1024,768]{1,0:T(8,128)(2,1)S(1)}, bf16[1024,768]{1,0:T(8,128)(2,1)}, u32[]{:S(2)}) copy-start(bf16[1024,768]{1,0:T(8,128)(2,1)} %copy-done.6) | copy-start | bytes 4718596
  79.4 14.4 %collective-permute-start = (bf16[768,768]{0,1:T(8,128)(2,1)}, bf16[768,768]{0,1:T(8,128)(2,1)}, u32[]{:S(2)}, u32[]{:S(2)}) collective-permute-start(bf16[768,768]{0,1:T(8,128)(2,1)} %add_convert_fusion.5), channel_id=1, source_target_pairs={{0,1},{2,3},{4,5},{6,7},{8,9},{10,11},{12,13},{14,15},{16,17},{18,... | collective-permute-start | bytes 3538952 | tf_op jit(solution)/shard_map/ppermute | solution.py:322
  89.5 10.4 %collective-permute-start.1 = (bf16[768,768]{0,1:T(8,128)(2,1)}, bf16[768,768]{0,1:T(8,128)(2,1)}, u32[]{:S(2)}, u32[]{:S(2)}) collective-permute-start(bf16[768,768]{0,1:T(8,128)(2,1)} %add_convert_fusion.4), channel_id=1, source_target_pairs={{0,1},{2,3},{4,5},{6,7},{8,9},{10,11},{12,13},{14,15},{16,17},{18,... | collective-permute-start | bytes 3538952 | tf_op jit(solution)/shard_map/ppermute | solution.py:322
  91.0 2.9 %copy-start.10 = (bf16[768,768]{0,1:T(8,128)(2,1)S(1)}, bf16[768,768]{0,1:T(8,128)(2,1)}, u32[]{:S(2)}) copy-start(bf16[768,768]{0,1:T(8,128)(2,1)} %copy.19) | copy-start | bytes 3538948
  93.8 2.9 %copy-start.8 = (bf16[1024,768]{1,0:T(8,128)(2,1)S(1)}, bf16[1024,768]{1,0:T(8,128)(2,1)}, u32[]{:S(2)}) copy-start(bf16[1024,768]{1,0:T(8,128)(2,1)} %copy-done.6) | copy-start | bytes 4718596
  96.7 3.2 %copy-start.13 = (bf16[768,768]{0,1:T(8,128)(2,1)S(1)}, bf16[768,768]{0,1:T(8,128)(2,1)}, u32[]{:S(2)}) copy-start(bf16[768,768]{0,1:T(8,128)(2,1)} %copy.21) | copy-start | bytes 3538948
  108.3 4.5 %copy-start.12 = (bf16[768,768]{0,1:T(8,128)(2,1)S(1)}, bf16[768,768]{0,1:T(8,128)(2,1)}, u32[]{:S(2)}) copy-start(bf16[768,768]{0,1:T(8,128)(2,1)} %copy.23) | copy-start | bytes 3538948
  112.8 9.1 %copy-start.16 = (f32[768]{0:T(1024)S(1)}, f32[768]{0:T(1024)}, u32[]{:S(2)}) copy-start(f32[768]{0:T(1024)} %param.19) | copy-start | bytes 9220
  (1 other events, 1.3 us)
where the time goes:
time: 126 us
  Pallas kernels  54.3 us (43%)
  matrix products  43.6 us (35%)
  other arithmetic  11.7 us (9%)
  local copies, waits for them, and re-layouts  11.5 us (9%)
  starting transfers between devices  4.15 us (3%)
    pallas_call x1, Pallas kernels, route(): pl.pallas_call(route_kernel, out_shape=(jax.ShapeDtypeStruct((2, SIDE, SI...  43.9 us
    dot_general x6, matrix products, dot_f32(): return jnp.dot(left_side, right_side, preferred_element_type=jnp.float32)  23.4 us
    dot_general x6, matrix products, contract_rows(): lax.dot_general(left_side, right_side, (((0,), (0,)), ((), ())), preferre...  16 us
    pallas_call x1, Pallas kernels, project(): pl.pallas_call(project_kernel, out_shape=(made, made, made), in_specs=[pl...  10.4 us
    unnamed x47, local copies, waits for them, and re-layouts  9.8 us
    convert_element_type x3, other arithmetic, fast_update(): (previous.astype(jnp.float32) + step_size * gradient * row_scale(gradient...  5.99 us
    ppermute x3, starting transfers between devices, body(): arrived = [lax.ppermute(w, 'ctx', [(0, 1)]) for w in updated]  4.15 us
    dot_general x2, matrix products, fast_update(): lax.dot_general(scaled_values, down_w, (((1,), (1,)), ((), ())), preferre...  4.13 us
  transfers between devices with their start and end apart: 3, of which 0 were waited for; matrix products, arithmetic and copies ran while one was open for 21% of the time, Pallas kernels for 0%

commit v1 on v0

--- a/solution.py
+++ b/solution.py
@@ -150,7 +150,7 @@
         route_kernel,
         out_shape=(
             jax.ShapeDtypeStruct((2, SIDE, SIDE, SIDE, BLK, width), jnp.bfloat16),
-            jax.ShapeDtypeStruct((SIDE, SIDE, SIDE, 1, 128), jnp.int32),
+            jax.ShapeDtypeStruct((SIDE, SIDE, SIDE, 2, 128), jnp.int32),
         ),
         in_specs=[
             pl.BlockSpec(memory_space=pltpu.SMEM),
@@ -176,114 +176,265 @@
     )(idx, meta, blocks)
 
 
-def project_kernel(meta_ref, buf_ref, wq_ref, wk_ref, wv_ref, rate_ref, q_ref, k_ref, v_ref, tokens, table, sems):
-    me = lax.axis_index("lane")
-    here = coords_of(me)
-
-    def place(s, p):
-        c = coords_of(s)
-        slot = lane_of([(h - o) % SIDE for h, o in zip(here, c)])
-        table[p] = slot
-        p = p + (meta_ref[s, 1] != me).astype(jnp.int32)
-        table[p] = s + LANES
-        return p + (meta_ref[s, 0] == me).astype(jnp.int32)
-
-    lax.fori_loop(0, LANES, place, jnp.int32(0))
-    chunk_blocks = 16
-    chunks = LANES // chunk_blocks
-
-    def fetch(r, carry):
-        pltpu.make_async_copy(buf_ref.at[table[r]], tokens.at[r], sems.at[r // chunk_blocks]).start()
-        return carry
-
-    lax.fori_loop(0, LANES, fetch, 0)
-
-    def project(c, carry):
-        span = pl.ds(c * chunk_blocks, chunk_blocks)
-        pltpu.make_async_copy(buf_ref.at[span], tokens.at[span], sems.at[c]).wait()
-        x = tokens[span].reshape(chunk_blocks * BLK, tokens.shape[2])
-        rows = pl.ds(c * chunk_blocks * BLK, chunk_blocks * BLK)
-        q = jnp.dot(x, wq_ref[...], preferred_element_type=jnp.float32)
-        q_ref[rows, :] = (q * row_scale(q)).astype(jnp.bfloat16)
-        k = jnp.dot(x, wk_ref[...], preferred_element_type=jnp.float32)
-        k_ref[rows, :] = (k * row_scale(k)).astype(jnp.bfloat16)
-        rate = jnp.dot(x, rate_ref[...], preferred_element_type=jnp.float32)
-        rate = jnp.maximum(rate, 0.0) + jnp.log1p(jnp.exp(-jnp.abs(rate)))
-        v = jnp.dot(x, wv_ref[...], preferred_element_type=jnp.float32)
-        v_ref[rows, :] = (rate[:, :1] * v).astype(jnp.bfloat16)
-        return carry
-
-    lax.fori_loop(0, chunks, project, 0)
+def dot_nn(left, right):
+    return jnp.dot(left, right, preferred_element_type=jnp.float32)
+
+
+def dot_nt(left, right):
+    return lax.dot_general(left, right, (((1,), (1,)), ((), ())), preferred_element_type=jnp.float32)
+
+
+def dot_tn(left, right):
+    return lax.dot_general(left, right, (((0,), (0,)), ((), ())), preferred_element_type=jnp.float32)
 
 
 def row_scale(values):
     return lax.rsqrt(jnp.mean(values * values, axis=-1, keepdims=True) + 1e-06)
 
 
-def project(meta, buf, w_query, w_key, w_value, rate):
+def order_row(meta, me):
+    source = lax.broadcasted_iota(jnp.int32, (LANES, 128), 0)
+    spot = lax.broadcasted_iota(jnp.int32, (LANES, 128), 1)
+    usual = (meta[1] != me).astype(jnp.int32)
+    double = (meta[0] == me).astype(jnp.int32)
+    upto = usual + double
+    shift = 1
+    while shift < LANES:
+        upto = upto + jnp.where(source >= shift, pltpu.roll(upto, shift, axis=0), 0)
+        shift *= 2
+    start = upto - usual - double
+    slot = (
+        ((me // 16 - source // 16) % SIDE) * 16
+        + ((me // 4 - source // 4) % SIDE) * 4
+        + (me - source) % SIDE
+    )
+    picks = jnp.where((usual == 1) & (start == spot), slot, 0)
+    picks = picks + jnp.where((double == 1) & (start + usual == spot), source + LANES, 0)
+    return jnp.sum(picks, axis=0, keepdims=True)
+
+
+def scene_kernel(meta_ref, buf_ref, wq_ref, wk_ref, wv_ref, rate_ref, gate_ref, up_ref, down_ref, gain_ref, out_ref,
+                 tokens, row_buf, table, queries, keys, values, term, hidden, grad, grad_down, gu_w, down_w,
+                 other_gu, other_down, sums, other_sums,
+                 sems, key_send, key_recv, val_send, val_recv, sum_send, sum_recv, w_send, w_recv):
+    me = lax.axis_index("lane")
+    ctx = lax.axis_index("ctx")
+    mate = (me, 1 - ctx)
+    width = tokens.shape[2]
+    half = width // 2
+    rows_all = LANES * BLK
+    chunk = 256
+    chunks = rows_all // chunk
+    blocks = chunk // BLK
+    step_size = 0.5 * width ** (-0.5)
+
+    barrier = pltpu.get_barrier_semaphore()
+    pl.semaphore_signal(barrier, inc=1, device_id=mate, device_id_type=MESH)
+
+    row_buf[...] = order_row([meta_ref[:, 0, :], meta_ref[:, 1, :]], me)
+    to_table = pltpu.make_async_copy(row_buf, table, sems)
+    to_table.start()
+    to_table.wait()
+
+    def fetch(r, carry):
+        tokens[r] = buf_ref[table[0, r]]
+        return carry
+
+    mine = pl.ds(pl.multiple_of(ctx * half, 128), half)
+    gu_w[0, pl.ds(0, half), :] = gate_ref[:, mine].T
+    gu_w[0, pl.ds(half, half), :] = up_ref[:, mine].T
+    down_w[0] = down_ref[mine, :]
+
+    def share(ref, send, recv, seg, c):
+        part = ref.at[seg, pl.ds(c * chunk, chunk)]
+        return pltpu.make_async_remote_copy(
+            src_ref=part, dst_ref=part, send_sem=send.at[c], recv_sem=recv.at[c],
+            device_id=mate, device_id_type=MESH)
+
+    pl.semaphore_wait(barrier, 1)
+
+    def load(c):
+        x = tokens[pl.ds(c * blocks, blocks)].reshape(chunk, width)
+        return x, pl.ds(c * chunk, chunk)
+
+    def project(c, carry):
+        lax.fori_loop(c * blocks, (c + 1) * blocks, fetch, 0)
+        x, rows = load(c)
+        k = dot_nn(x, wk_ref[...])
+        keys[ctx, rows, :] = (k * row_scale(k)).astype(jnp.bfloat16)
+        share(keys, key_send, key_recv, ctx, c).start()
+        rate = dot_nn(x, rate_ref[...])
+        rate = jnp.maximum(rate, 0.0) + jnp.log1p(jnp.exp(-jnp.abs(rate)))
+        v = dot_nn(x, wv_ref[...])
+        values[ctx, rows, :] = (rate[:, :1] * v).astype(jnp.bfloat16)
+        share(values, val_send, val_recv, ctx, c).start()
+        return carry
+
+    lax.fori_loop(0, chunks, project, 0)
+
+    def ask(c, carry):
+        x, rows = load(c)
+        q = dot_nn(x, wq_ref[...])
+        queries[rows, :] = (q * row_scale(q)).astype(jnp.bfloat16)
+        return carry
+
+    lax.fori_loop(0, chunks, ask, 0)
+
+    def arrived():
+        def one(c, carry):
+            share(keys, key_send, key_recv, 1 - ctx, c).wait_recv()
+            share(values, val_send, val_recv, 1 - ctx, c).wait_recv()
+            return carry
+
+        lax.fori_loop(0, chunks, one, 0)
+
+    def share_sums(seg):
+        return pltpu.make_async_remote_copy(
+            src_ref=sums.at[seg], dst_ref=other_sums.at[seg], send_sem=sum_send.at[seg], recv_sem=sum_recv.at[seg],
+            device_id=mate, device_id_type=MESH)
+
+    def share_weights(seg):
+        return (
+            pltpu.make_async_remote_copy(
+                src_ref=gu_w.at[seg + 1], dst_ref=other_gu, send_sem=w_send.at[0], recv_sem=w_recv.at[0],
+                device_id=mate, device_id_type=MESH),
+            pltpu.make_async_remote_copy(
+                src_ref=down_w.at[seg + 1], dst_ref=other_down, send_sem=w_send.at[1], recv_sem=w_recv.at[1],
+                device_id=mate, device_id_type=MESH),
+        )
+
+    def update(seg):
+        def terms(c, carry):
+            rows = pl.ds(c * chunk, chunk)
+            pre = dot_nt(keys[seg, rows, :], gu_w[seg])
+            back = dot_nt(values[seg, rows, :], down_w[seg])
+            gate_pre, up_pre = pre[:, :half], pre[:, half:]
+            gate_sig = jax.nn.sigmoid(gate_pre)
+            gated = gate_pre * gate_sig
+            hidden[rows, :] = (gated * up_pre).astype(jnp.bfloat16)
+            term[rows, pl.ds(0, half)] = (
+                back * up_pre * gate_sig * (1.0 + gate_pre * (1.0 - gate_sig))
+            ).astype(jnp.bfloat16)
+            term[rows, pl.ds(half, half)] = (back * gated).astype(jnp.bfloat16)
+            return carry
+
+        lax.fori_loop(0, chunks, terms, 0)
+
+        def slopes(j, carry):
+            cols = pl.ds(pl.multiple_of(j * half, 128), half)
+            g = dot_tn(term[:, cols], keys[seg])
+            grad[pl.ds(j * half, half), :] = g
+            sums[seg, pl.ds(j, 1), :] = jnp.sum(g * g, axis=0, keepdims=True)
+            return carry
+
+        lax.fori_loop(0, 2, slopes, 0)
+        share_sums(seg).start()
+        grad_down[...] = dot_tn(hidden[...], values[seg])
+        g = grad_down[...]
+        down_w[seg + 1] = (
+            down_w[seg].astype(jnp.float32) + step_size * g * row_scale(g)
+        ).astype(jnp.bfloat16)
+        share_sums(seg).wait_recv()
+        for j in range(2):
+            rows = pl.ds(j * half, half)
+            total = sums[seg, pl.ds(j, 1), :] + other_sums[seg, pl.ds(j, 1), :]
+            scale = step_size * lax.rsqrt(total * (1.0 / width) + 1e-06)
+            gu_w[seg + 1, rows, :] = (
+                gu_w[seg, rows, :].astype(jnp.float32) + grad[rows, :] * scale
+            ).astype(jnp.bfloat16)
+
+    @pl.when(ctx == 1)
+    def _():
+        arrived()
+
+    update(0)
+
+    @pl.when(ctx == 1)
+    def _():
+        for copy in share_weights(0):
+            copy.start()
+
+    @pl.when(ctx == 0)
+    def _():
+        arrived()
+
+    update(1)
+
+    @pl.when(ctx == 0)
+    def _():
+        for copy in share_weights(1):
+            copy.start()
+
+    def answer_half(rows, gu):
+        pre = dot_nt(queries[rows, :], gu)
+        q_gate, q_up = pre[:, :half], pre[:, half:]
+        return (q_gate * jax.nn.sigmoid(q_gate) * q_up).astype(jnp.bfloat16)
+
+    def answer_own(c, carry):
+        rows = pl.ds(c * chunk, chunk)
+        hidden[rows, :] = answer_half(rows, gu_w[ctx + 1])
+        return carry
+
+    lax.fori_loop(0, chunks, answer_own, 0)
+    for copy in share_weights(0):
+        copy.wait_recv()
+
+    def answer(c, carry):
+        rows = pl.ds(c * chunk, chunk)
+        y = dot_nn(hidden[rows, :], down_w[ctx + 1])
+        y = y + dot_nn(answer_half(rows, other_gu[...]), other_down[...])
+        out_ref[rows, :] = (y * row_scale(y) * gain_ref[...]).astype(jnp.bfloat16)
+        return carry
+
+    lax.fori_loop(0, chunks, answer, 0)
+
+    def sent(c, carry):
+        share(keys, key_send, key_recv, ctx, c).wait_send()
+        share(values, val_send, val_recv, ctx, c).wait_send()
+        return carry
+
+    lax.fori_loop(0, chunks, sent, 0)
+    for seg in range(2):
+        share_sums(seg).wait_send()
+    for copy in share_weights(0):
+        copy.wait_send()
+
+
+def scene(meta, buf, *operands):
     width = buf.shape[2]
     rows = LANES * BLK
-    made = jax.ShapeDtypeStruct((rows, width), jnp.bfloat16)
+    half = width // 2
     vmem = pl.BlockSpec(memory_space=pltpu.VMEM)
+    bf, f32, dma = jnp.bfloat16, jnp.float32, pltpu.SemaphoreType.DMA
     return pl.pallas_call(
-        project_kernel,
-        out_shape=(made, made, made),
-        in_specs=[pl.BlockSpec(memory_space=pltpu.SMEM), pl.BlockSpec(memory_space=pl.ANY), vmem, vmem, vmem, vmem],
-        out_specs=(vmem, vmem, vmem),
+        scene_kernel,
+        out_shape=jax.ShapeDtypeStruct((rows, width), bf),
+        in_specs=[vmem] * (2 + len(operands)),
+        out_specs=vmem,
         scratch_shapes=[
-            pltpu.VMEM((LANES, BLK, width), jnp.bfloat16),
-            pltpu.SMEM((LANES + 8,), jnp.int32),
-            pltpu.SemaphoreType.DMA((4,)),
+            pltpu.VMEM((LANES, BLK, width), bf),
+            pltpu.VMEM((1, 128), jnp.int32),
+            pltpu.SMEM((1, 128), jnp.int32),
+            pltpu.VMEM((rows, width), bf),
+            pltpu.VMEM((2, rows, width), bf),
+            pltpu.VMEM((2, rows, width), bf),
+            pltpu.VMEM((rows, width), bf),
+            pltpu.VMEM((rows, half), bf),
+            pltpu.VMEM((width, width), f32),
+            pltpu.VMEM((half, width), f32),
+            pltpu.VMEM((3, width, width), bf),
+            pltpu.VMEM((3, half, width), bf),
+            pltpu.VMEM((width, width), bf),
+            pltpu.VMEM((half, width), bf),
+            pltpu.VMEM((2, 8, width), f32),
+            pltpu.VMEM((2, 8, width), f32),
+            dma, dma((4,)), dma((4,)), dma((4,)), dma((4,)), dma((2,)), dma((2,)), dma((2,)), dma((2,)),
         ],
-        compiler_params=pltpu.CompilerParams(vmem_limit_bytes=40 << 20),
-        name="project",
-    )(meta, buf, w_query, w_key, w_value, rate)
-
-
-def dot_f32(left_side, right_side):
-    return jnp.dot(left_side, right_side, preferred_element_type=jnp.float32)
-
-
-def contract_rows(left_side, right_side):
-    return lax.dot_general(
-        left_side, right_side, (((0,), (0,)), ((), ())), preferred_element_type=jnp.float32
-    )
-
-
-def fast_update(gate_w, up_w, down_w, keys_bf, scaled_values):
-    gate_pre = dot_f32(keys_bf, gate_w)
-    up_pre = dot_f32(keys_bf, up_w)
-    gate_sig = jax.nn.sigmoid(gate_pre)
-    hidden = (gate_pre * gate_sig * up_pre).astype(jnp.bfloat16)
-    back = lax.dot_general(
-        scaled_values, down_w, (((1,), (1,)), ((), ())), preferred_element_type=jnp.float32
-    )
-    gate_term = (back * up_pre * gate_sig * (1.0 + gate_pre * (1.0 - gate_sig))).astype(
-        jnp.bfloat16
-    )
-    up_term = (back * gate_pre * gate_sig).astype(jnp.bfloat16)
-    gradients = (
-        contract_rows(keys_bf, gate_term),
-        contract_rows(keys_bf, up_term),
-        contract_rows(hidden, scaled_values),
-    )
-    step_size = 0.5 * gate_w.shape[0] ** (-0.5)
-    renewed = []
-    for previous, gradient in zip((gate_w, up_w, down_w), gradients):
-        renewed.append(
-            (previous.astype(jnp.float32) + step_size * gradient * row_scale(gradient)).astype(
-                jnp.bfloat16
-            )
-        )
-    return tuple(renewed)
-
-
-def apply_queries(gate_w, up_w, down_w, queries_bf, out_gain):
-    q_gate = dot_f32(queries_bf, gate_w)
-    q_up = dot_f32(queries_bf, up_w)
-    q_hidden = (jax.nn.silu(q_gate) * q_up).astype(jnp.bfloat16)
-    output_pre = dot_f32(q_hidden, down_w)
-    return (output_pre * row_scale(output_pre) * out_gain).astype(jnp.bfloat16)
+        compiler_params=pltpu.CompilerParams(
+            collective_id=1, has_side_effects=True, vmem_limit_bytes=56 << 20
+        ),
+        name="scene",
+    )(meta, buf, *operands)
 
 
 def body(
@@ -298,7 +449,6 @@
     fast_down,
     out_gain,
 ):
-    position = lax.axis_index("ctx")
     width = view_tokens.shape[2]
     blocks = view_tokens[0].reshape(LANES, BLK, width)
     lane_ids = jnp.arange(LANES, dtype=jnp.int32)
@@ -311,18 +461,14 @@
     missed = jnp.max(jnp.where(first == LANES, lane_ids, -1))
     columns = jnp.arange(128, dtype=jnp.int32)
     idx = jnp.where(columns < LANES, jnp.pad(jnp.minimum(first, LANES - 1), (0, 64)), extra)
-    meta = jnp.where(columns == 0, doubled, missed)[None, :]
+    meta = jnp.broadcast_to(jnp.stack([doubled, missed])[:, None], (2, 128))
     buf, all_meta = route(idx, meta, blocks)
     rate = jnp.broadcast_to(rate_vector[:, None], (width, 128))
-    queries, keys, values = project(
-        all_meta.reshape(LANES, 128), buf.reshape(2 * LANES, BLK, width), w_query, w_key, w_value, rate
+    out = scene(
+        all_meta.reshape(LANES, 2, 128), buf.reshape(2 * LANES, BLK, width), w_query, w_key, w_value, rate,
+        fast_gate, fast_up, fast_down, out_gain[None, :]
     )
-    initial = (fast_gate, fast_up, fast_down)
-    updated = fast_update(*initial, keys, values)
-    arrived = [lax.ppermute(w, "ctx", [(0, 1)]) for w in updated]
-    weights = [jnp.where(position == 0, a, b) for a, b in zip(initial, arrived)]
-    weights = fast_update(*weights, keys, values)
-    return apply_queries(*weights, queries, out_gain)[None]
+    return out[None]
 
 
 def solution(mesh):

time: 126 us -> 92.5 us (0.73)
  matrix products: 43.6 us -> 0 us
  Pallas kernels: 54.3 us -> 79.5 us
  other arithmetic: 11.7 us -> 3.44 us
  starting transfers between devices: 4.15 us -> 0 us
  local copies, waits for them, and re-layouts: 11.5 us -> 9.19 us
    dot_general x14 -> x0, matrix products: 43.6 us -> none  [the longest x6 23.4 us: dot_f32(): return jnp.dot(left_side, right_side, preferred_element_type=jnp.float32)]
    pallas_call x1, Pallas kernels: 10.4 us -> 35.7 us  [scene(): pl.pallas_call(scene_kernel, out_shape=jax.ShapeDtypeStruct((rows, width)...]
    convert_element_type x3 -> x0, other arithmetic: 5.99 us -> none  [fast_update(): (previous.astype(jnp.float32) + step_size * gradient * row_scale(gradient...]
    ppermute x3 -> x0, starting transfers between devices: 4.15 us -> none  [body(): arrived = [lax.ppermute(w, 'ctx', [(0, 1)]) for w in updated]]
    unnamed x47 -> x7, local copies, waits for them, and re-layouts: 9.8 us -> 6.33 us
    broadcast_in_dim x1 -> x0, other arithmetic: 2.21 us -> none  [body(): return apply_queries(*weights, queries, out_gain)[None]]
    broadcast_in_dim x1, local copies, waits for them, and re-layouts: 0.16 us -> 1.53 us  [body(): rate = jnp.broadcast_to(rate_vector[:, None], (width, 128))]
    select_n x1 -> x0, other arithmetic: 1.28 us -> none  [body(): meta = jnp.where(columns == 0, doubled, missed)[None, :]]
  transfers between devices with their start and end apart: 3 -> 0, of which waited for: 0 -> 0; matrix products, arithmetic and copies ran while one was open for 21% -> 0% of each run, Pallas kernels for 0% -> 0%
where the time goes in v1:
time: 92.5 us; the launch traced here: 92.2 us
  Pallas kernels  79.5 us (86%)
  local copies, waits for them, and re-layouts  9.19 us (10%)
  other arithmetic  3.44 us (4%)
    pallas_call x1, Pallas kernels, route(): pl.pallas_call(route_kernel, out_shape=(jax.ShapeDtypeStruct((2, SIDE, SI...  43.8 us
    pallas_call x1, Pallas kernels, scene(): pl.pallas_call(scene_kernel, out_shape=jax.ShapeDtypeStruct((rows, width)...  35.7 us
    unnamed x7, local copies, waits for them, and re-layouts  6.33 us

profile of v1, /device:TPU:1, one launch (start us, length us, event | category | flops | bytes accessed | tf_op | source)
XLA Modules:
  0.0 92.2 jit_solution(3631819653515144148)
XLA Ops:
  0.0 0.7 select_reduce_fusion
  0.7 0.7 fusion.1
  1.5 0.7 compare_select_fusion.1.idx_ref
  2.2 1.3 %pad_add_fusion = s32[2]{0:T(128)S(1)} fusion(s32[1]{0:T(128)} %bitcast.2, s32[1]{0:T(128)} %bitcast.1), kind=kLoop, calls=%fused_computation.10 | loop fusion | flops 2 | bytes 16 | tf_op jit(solution)/shard_map/stack | solution.py:464
  3.4 0.1 broadcast_in_dim.57.meta_ref
  3.5 1.3 %broadcast_in_dim.59.gain_ref = f32[1,768]{1,0:T(1,128)} reshape(f32[768]{0:T(1024)} %param.19) | data formatting | bytes 6144 | tf_op jit(solution)/shard_map/broadcast_in_dim | solution.py:469
  4.8 1.5 %broadcast_in_dim.58.rate_ref = bf16[768,128]{1,0:T(8,128)(2,1)} broadcast(bf16[768]{0:T(1024)(128)(2,1)} %param.15), dimensions={0} | broadcast | bytes 198144 | tf_op jit(solution)/shard_map/broadcast_in_dim | solution.py:466
  6.3 0.0 copy-start.1
  6.3 1.4 %copy-done.1 = bf16[1,1024,768]{2,1,0:T(8,128)(2,1)S(1)} copy-done((bf16[1,1024,768]{2,1,0:T(8,128)(2,1)S(1)}, bf16[1,1024,768]{2,1,0:T(8,128)(2,1)}, u32[]{:S(2)}) %copy-start.1) | copy-done | bytes 1572888
  7.7 43.8 %route.1 = (bf16[2,4,4,4,16,768]{5,4,3,2,1,0:T(8,128)(2,1)S(1)}, s32[4,4,4,2,128]{4,3,2,1,0:T(2,128)S(1)}) custom-call(s32[128]{0:T(128)S(1)} %compare_select_fusion.1.idx_ref, s32[2,128]{1,0:T(2,128)S(1)} %broadcast_in_dim.57.meta_ref, bf16[64,16,768]{2,1,0:T(8,128)(2,1)S(1)} %bitcast.8), custom_call_target="tpu_custom_call" | custom-call | tf_op jit(solution)/shard_map/route/pallas_call | solution.py:149
  51.5 0.0 copy-start
  51.5 1.7 %copy-done = bf16[2,4,4,4,16,768]{5,4,3,2,1,0:T(8,128)(2,1)} copy-done((bf16[2,4,4,4,16,768]{5,4,3,2,1,0:T(8,128)(2,1)}, bf16[2,4,4,4,16,768]{5,4,3,2,1,0:T(8,128)(2,1)S(1)}, u32[]{:S(2)}) %copy-start) | copy-done | bytes 3145752
  53.2 0.0 copy-start.2
  53.2 0.6 copy-done.2
  53.8 35.7 %scene.1 = bf16[1024,768]{1,0:T(8,128)(2,1)} custom-call(s32[64,2,128]{2,1,0:T(2,128)} %bitcast.9, bf16[128,16,768]{2,1,0:T(8,128)(2,1)} %bitcast.7, bf16[768,768]{1,0:T(8,128)(2,1)} %wq_ref.1, bf16[768,768]{1,0:T(8,128)(2,1)} %wk_ref.1, bf16[768,768]{1,0:T(8,128)(2,1)} %wv_ref.1, bf16[768,128]{1,0:T(8,128)(2,1)} %broadcast_in_dim.58.rate_ref, ...), custom_call_target="tpu_custom_call" | custom-call | tf_op jit(solution)/shard_map/scene/pallas_call | solution.py:409
  89.6 2.7 %copy.12 = bf16[1,1024,768]{2,1,0:T(8,128)(2,1)} copy(bf16[1,1024,768]{2,1,0:T(8,128)(2,1)} %bitcast.10) | data formatting | bytes 3145728
Async XLA Ops:
  6.3 1.4 %copy-start.1 = (bf16[1,1024,768]{2,1,0:T(8,128)(2,1)S(1)}, bf16[1,1024,768]{2,1,0:T(8,128)(2,1)}, u32[]{:S(2)}) copy-start(bf16[1,1024,768]{2,1,0:T(8,128)(2,1)} %param.10) | copy-start | bytes 4718596
  51.5 1.7 %copy-start = (bf16[2,4,4,4,16,768]{5,4,3,2,1,0:T(8,128)(2,1)}, bf16[2,4,4,4,16,768]{5,4,3,2,1,0:T(8,128)(2,1)S(1)}, u32[]{:S(2)}) copy-start(bf16[2,4,4,4,16,768]{5,4,3,2,1,0:T(8,128)(2,1)S(1)} %get-tuple-element.8) | copy-start | bytes 9437188
  53.2 0.6 copy-start.2
